TPU v7x, 32 devices: a whole 2x2x4 slice. The times are simulated.
32 devices in a mesh: shard: 8 (over y, x, core), rep: 4 (over z).
Axes of the slice: x: 2, y: 2, z: 4, core: 2. Of those that a mesh axis runs over, the one named last changes fastest.
Arguments:
- inputs: bfloat16 [64, 256, 1024], P(('shard', 'rep')), may hold values from -6 to 6
- lengths: int32 [64], replicated, may hold values from 64 to 256, as said below
- dealing: int32 [64], replicated, may hold values from 0 to 63, as said below
- w_query: bfloat16 [1024, 1024], P('shard'), may hold values from -0.25 to 0.25
- w_key: bfloat16 [1024, 1024], P('shard'), may hold values from -0.25 to 0.25
- w_value: bfloat16 [1024, 1024], P('shard'), may hold values from -0.1875 to 0.1875
- w_out: bfloat16 [1024, 1024], P('shard'), may hold values from -0.5 to 0.5
- b_query: bfloat16 [1024], P('shard'), may hold values from -1.5 to 1.5
- b_value: bfloat16 [1024], P('shard'), may hold values from -1.5 to 1.5
- b_out: bfloat16 [1024], P('shard'), may hold values from -1.5 to 1.5
- ln1_gain: bfloat16 [1024], P('shard'), may hold values from 0.099609375 to 1.8984375
- ln1_bias: bfloat16 [1024], P('shard'), may hold values from -1.5 to 1.5
- w_up: bfloat16 [1024, 4096], P('shard'), may hold values from -0.1875 to 0.1875
- b_up: bfloat16 [4096], P('shard'), may hold values from -1.5 to 1.5
- w_down: bfloat16 [4096, 1024], P('shard'), may hold values from -0.09375 to 0.09375
- b_down: bfloat16 [1024], P('shard'), may hold values from -1.5 to 1.5
- ln2_gain: bfloat16 [1024], P('shard'), may hold values from 0.099609375 to 1.8984375
- ln2_bias: bfloat16 [1024], P('shard'), may hold values from -1.5 to 1.5
- cotangent: bfloat16 [64, 256, 1024], P(('shard', 'rep')), may hold values from -6 to 6
Outputs:
- layer_out: bfloat16 [64, 256, 1024], P(('shard', 'rep'))
- grad_input: bfloat16 [64, 256, 1024], P(('shard', 'rep'))
- grad_w_query: float32 [1024, 1024], P('shard')
- grad_w_key: float32 [1024, 1024], P('shard')
- grad_w_value: float32 [1024, 1024], P('shard')
- grad_w_out: float32 [1024, 1024], P('shard')
- grad_b_query: float32 [1024], P('shard')
- grad_b_value: float32 [1024], P('shard')
- grad_b_out: float32 [1024], P('shard')
- grad_ln1_gain: float32 [1024], P('shard')
- grad_ln1_bias: float32 [1024], P('shard')
- grad_w_up: float32 [1024, 4096], P('shard')
- grad_b_up: float32 [4096], P('shard')
- grad_w_down: float32 [4096, 1024], P('shard')
- grad_b_down: float32 [1024], P('shard')
- grad_ln2_gain: float32 [1024], P('shard')
- grad_ln2_bias: float32 [1024], P('shard')
Inputs may be any that keep to these rules, and one draw needn't show every extreme that they name: `lengths`: length of initial sequence; positions at or past it are padding. `dealing`: a permutation of the 64 sequences that maps each aligned block of 8 positions onto itself.
All inputs are finite; a program needn't handle non-finite values.
Results may differ from a plain program's by a relative error of at most 0.02.
Values may be sent and summed in bfloat16 or wider, within the bound.
No kernel may reach another device: no remote copies, remote signals or barrier semaphores. Data moves between devices by JAX's collectives and lax.ppermute only.
A program may use at most 192 MiB of HBM per device.

v0:
```python
import jax
import jax.numpy as jnp
from jax import lax
from jax.sharding import PartitionSpec as P

H = 16
HD = 64
EPS = 1e-05
NEG = -1e30
F32 = jnp.float32
BF16 = jnp.bfloat16


def matmul(left, right):
    return jnp.dot(left, right, preferred_element_type=F32)


def left_trans(left, right):
    return lax.dot_general(left, right, (((0,), (0,)), ((), ())), preferred_element_type=F32)


def right_trans(left, right):
    return lax.dot_general(left, right, (((1,), (1,)), ((), ())), preferred_element_type=F32)


def normalize(values, gain, shift):
    center = values - jnp.mean(values, -1, keepdims=True)
    inverse = lax.rsqrt(jnp.mean(center * center, -1, keepdims=True) + EPS)
    unit = center * inverse
    return (unit * gain + shift, unit, inverse)


def norm_back(grad, unit, inverse, gain):
    scaled = grad * gain
    return inverse * (
        scaled
        - jnp.mean(scaled, -1, keepdims=True)
        - unit * jnp.mean(scaled * unit, -1, keepdims=True)
    )


def gelu_both(pre):
    cumul = 0.5 * (1.0 + lax.erf(pre * 0.7071067811865476))
    density = jnp.exp(-0.5 * pre * pre) * 0.3989422804014327
    return (pre * cumul, cumul + pre * density)


def pick(pool, targets):
    return jnp.stack(
        [
            lax.dynamic_index_in_dim(pool, targets[i], 0, keepdims=False)
            for i in range(targets.shape[0])
        ]
    )


def local(
    inputs,
    lengths,
    dealing,
    w_query,
    w_key,
    w_value,
    w_out,
    b_query,
    b_value,
    b_out,
    ln1_gain,
    ln1_bias,
    w_up,
    b_up,
    w_down,
    b_down,
    ln2_gain,
    ln2_bias,
    cotangent,
):
    batches, rows, width = inputs.shape
    shards = lax.axis_size("shard")
    replicas = lax.axis_size("rep")
    group = batches * replicas
    shard_index = lax.axis_index("shard")
    rep_index = lax.axis_index("rep")
    anchor = shard_index * group
    slots = anchor + rep_index * batches + jnp.arange(batches, dtype=jnp.int32)
    seq_lengths = jnp.take(lengths, slots)
    local_dealing = lax.dynamic_slice_in_dim(dealing, anchor, group) - anchor
    sources = jnp.take(dealing, slots) - anchor
    places = jnp.arange(group, dtype=jnp.int32)
    wanted = jnp.sum(
        jnp.where(local_dealing[None, :] == (slots - anchor)[:, None], places[None, :], 0), 1
    )

    def gather(block):
        return lax.all_gather(block, "shard", axis=0, tiled=True)

    block = w_query.shape[0]
    wide = w_up.shape[1]
    small = (b_query, b_value, b_out, ln1_gain, ln1_bias, b_down, ln2_gain, ln2_bias, b_up)
    vec = jnp.concatenate(small)
    first = jnp.concatenate([w_query, w_key, w_value, w_out], 0)
    all_vec = lax.all_gather(vec, "shard", axis=0, tiled=True).reshape(shards, -1)
    all_first = gather(first).reshape(shards, 4, block, width)
    cuts = [0]
    for part in small:
        cuts.append(cuts[-1] + part.shape[0])
    (
        bias_query,
        bias_value,
        bias_out,
        gain_one,
        shift_one,
        bias_down,
        gain_two,
        shift_two,
        bias_up,
    ) = [all_vec[:, cuts[i] : cuts[i + 1]].reshape(-1).astype(F32) for i in range(len(small))]
    full_query, full_key, full_value, full_out = [
        all_first[:, i].reshape(width, width) for i in range(4)
    ]
    full_up = gather(w_up)
    full_down = gather(w_down)
    cot = pick(lax.all_gather(cotangent, "rep", axis=0, tiled=True), wanted)
    tokens = inputs.reshape(batches * rows, width)
    query = (matmul(tokens, full_query) + bias_query).astype(BF16)
    keyed = matmul(tokens, full_key).astype(BF16)
    value = (matmul(tokens, full_value) + bias_value).astype(BF16)
    heads = lambda a: a.reshape(batches, rows, H, HD).transpose(0, 2, 1, 3)
    flat = lambda a: a.transpose(0, 2, 1, 3).reshape(batches * rows, width)
    qh, kh, vh = (heads(query), heads(keyed), heads(value))
    allowed = (
        lax.broadcasted_iota(jnp.int32, (batches, 1, 1, rows), 3) < seq_lengths[:, None, None, None]
    )
    scale = HD ** (-0.5)
    scores = jnp.einsum("bhqd,bhkd->bhqk", qh, kh, preferred_element_type=F32) * scale
    scores = jnp.where(allowed, scores, NEG)
    raised = jnp.exp(scores - jnp.max(scores, -1, keepdims=True))
    probs = raised / jnp.sum(raised, -1, keepdims=True)
    probs_low = probs.astype(BF16)
    mixed_low = flat(
        jnp.einsum("bhqk,bhkd->bhqd", probs_low, vh, preferred_element_type=F32).astype(BF16)
    )
    hidden, unit_one, inverse_one = normalize(
        tokens.astype(F32) + matmul(mixed_low, full_out) + bias_out, gain_one, shift_one
    )
    hidden_low = hidden.astype(BF16)
    pre = matmul(hidden_low, full_up) + bias_up
    act, slope = gelu_both(pre)
    act_low = act.astype(BF16)
    summed = hidden + matmul(act_low, full_down) + bias_down
    normed, unit_two, inverse_two = normalize(summed, gain_two, shift_two)
    valid = (
        lax.broadcasted_iota(jnp.int32, (batches, rows, 1), 1) < seq_lengths[:, None, None]
    ).reshape(-1, 1)
    out = jnp.where(valid, normed, 0.0).astype(BF16).reshape(batches, rows, width)
    layer_out = pick(lax.all_gather(out, "rep", axis=0, tiled=True), sources)
    grad_out = jnp.where(valid, cot.reshape(-1, width).astype(F32), 0.0)
    grad_gain_two = jnp.sum(grad_out * unit_two, 0)
    grad_shift_two = jnp.sum(grad_out, 0)
    grad_sum = norm_back(grad_out, unit_two, inverse_two, gain_two)
    grad_bias_down = jnp.sum(grad_sum, 0)
    grad_sum_low = grad_sum.astype(BF16)

    def reduced(part):
        return lax.psum_scatter(part, "shard", scatter_dimension=0, tiled=True)

    def over_rep(part):
        return lax.psum(part, "rep").astype(F32)

    g_down = reduced(left_trans(act_low, grad_sum_low).astype(BF16))
    grad_pre = (right_trans(grad_sum_low, full_down) * slope).astype(BF16)
    grad_bias_up = jnp.sum(grad_pre.astype(F32), 0)
    g_up = reduced(left_trans(hidden_low, grad_pre).astype(BF16))
    grad_hidden = grad_sum + right_trans(grad_pre, full_up)
    grad_gain_one = jnp.sum(grad_hidden * unit_one, 0)
    grad_shift_one = jnp.sum(grad_hidden, 0)
    grad_resid = norm_back(grad_hidden, unit_one, inverse_one, gain_one)
    grad_bias_out = jnp.sum(grad_resid, 0)
    grad_resid_low = grad_resid.astype(BF16)
    grad_w_out = left_trans(mixed_low, grad_resid_low).astype(BF16)
    grad_mixed = heads(right_trans(grad_resid_low, full_out).astype(BF16))
    grad_probs = jnp.einsum("bhqd,bhkd->bhqk", grad_mixed, vh, preferred_element_type=F32)
    inner = jnp.sum(probs * grad_probs, -1, keepdims=True)
    grad_scores = (probs * (grad_probs - inner) * scale).astype(BF16)
    query_low = flat(
        jnp.einsum("bhqk,bhkd->bhqd", grad_scores, kh, preferred_element_type=F32).astype(BF16)
    )
    key_low = flat(
        jnp.einsum("bhqk,bhqd->bhkd", grad_scores, qh, preferred_element_type=F32).astype(BF16)
    )
    value_low = flat(
        jnp.einsum("bhqk,bhqd->bhkd", probs_low, grad_mixed, preferred_element_type=F32).astype(
            BF16
        )
    )
    grad_bias_query = jnp.sum(query_low.astype(F32), 0)
    grad_bias_value = jnp.sum(value_low.astype(F32), 0)
    blocks = [
        part.reshape(shards, block, width)
        for part in (
            left_trans(tokens, query_low).astype(BF16),
            left_trans(tokens, key_low).astype(BF16),
            left_trans(tokens, value_low).astype(BF16),
            grad_w_out,
        )
    ]
    g_first = reduced(jnp.concatenate(blocks, 1).reshape(shards * 4 * block, width))
    grad_tokens = (
        grad_resid
        + right_trans(query_low, full_query)
        + right_trans(key_low, full_key)
        + right_trans(value_low, full_value)
    )
    grad_input = grad_tokens.astype(BF16).reshape(batches, rows, width)
    vec_terms = (
        grad_bias_query,
        grad_bias_value,
        grad_bias_out,
        grad_gain_one,
        grad_shift_one,
        grad_bias_down,
        grad_gain_two,
        grad_shift_two,
        grad_bias_up,
    )
    g_vec = jnp.concatenate([part.reshape(shards, -1) for part in vec_terms], 1)
    g_vec = lax.psum(g_vec, ("shard", "rep"))
    g_vec = lax.dynamic_index_in_dim(g_vec, shard_index, 0, keepdims=False)
    g_bquery, g_bvalue, g_bout, g_gain_one, g_shift_one, g_bdown, g_gain_two, g_shift_two, g_bup = [
        g_vec[cuts[i] : cuts[i + 1]] for i in range(len(small))
    ]
    g_down = over_rep(g_down)
    g_up = over_rep(g_up)
    g_first = over_rep(g_first).reshape(4, block, width)
    return (
        layer_out,
        grad_input,
        g_first[0],
        g_first[1],
        g_first[2],
        g_first[3],
        g_bquery,
        g_bvalue,
        g_bout,
        g_gain_one,
        g_shift_one,
        g_up,
        g_bup,
        g_down,
        g_bdown,
        g_gain_two,
        g_shift_two,
    )


def solution(mesh):
    seqs = P(("shard", "rep"), None, None)
    mat = P("shard", None)
    vec = P("shard")
    in_specs = (
        seqs,
        P(),
        P(),
        mat,
        mat,
        mat,
        mat,
        vec,
        vec,
        vec,
        vec,
        vec,
        mat,
        vec,
        mat,
        vec,
        vec,
        vec,
        seqs,
    )
    out_specs = (
        seqs,
        seqs,
        mat,
        mat,
        mat,
        mat,
        vec,
        vec,
        vec,
        vec,
        vec,
        mat,
        vec,
        mat,
        vec,
        vec,
        vec,
    )
    return jax.shard_map(local, mesh=mesh, in_specs=in_specs, out_specs=out_specs, check_vma=False)
```

profile of v0, /device:TPU:0, one launch (start us, length us, event | category | flops | bytes accessed | tf_op | source)
XLA Modules:
  0.0 790.4 jit_solution(13564791712874749416)
XLA Ops:
  8.0 2.2 pad_maximum_fusion.1
  18.1 10.6 %all-gather = bf16[8,1,1536]{2,1,0:T(2,128)(2,1)S(1)} all-gather(bf16[1,1,1536]{2,1,0:T(2,128)(2,1)S(1)} %reshape.383), channel_id=1, replica_groups=mesh['shard'=8,'rep'=4] {'shard'}, dimensions={0}, use_global_device_ids=true | all-gather | bytes 27648 | tf_op jit(solution)/shard_map/all_gather | solution.py:102
  30.9 62.3 %all-gather.15.cloned.1.call-done = bf16[8,256,1024]{2,1,0:T(8,128)(2,1)} async-done(((bf16[2,256,1024]{2,1,0:T(8,128)(2,1)}), bf16[8,256,1024]{2,1,0:T(8,128)(2,1)}) %all-gather.15.cloned.1.call-update) | async-done | bytes 4194320 | tf_op jit(solution)/shard_map/all_gather | solution.py:123
  95.5 53.0 %all-gather.7.cloned.1.call-done = bf16[4096,1024]{1,0:T(8,128)(2,1)} async-done(((bf16[512,1024]{1,0:T(8,128)(2,1)}), bf16[4096,1024]{1,0:T(8,128)(2,1)}) %all-gather.7.cloned.1.call-update) | async-done | bytes 8388624 | tf_op jit(solution)/shard_map/all_gather | solution.py:95
  148.5 5.9 fusion.97
  154.4 1.3 copy-done.6
  155.8 1.3 fusion.54
  157.4 4.7 fusion.43
  162.1 1.3 reshape.332
  163.5 4.5 fusion.53
  168.0 2.1 reshape.331
  170.1 2.5 fusion.59
  172.6 3.5 fusion.101
  177.0 3.3 copy-done.41
  182.2 1.4 fusion.102
  183.9 20.9 %all-gather.9.cloned.1.call-done = bf16[1024,4096]{1,0:T(8,128)(2,1)} async-done(((bf16[128,4096]{1,0:T(8,128)(2,1)}), bf16[1024,4096]{1,0:T(8,128)(2,1)}) %all-gather.9.cloned.1.call-update) | async-done | bytes 8388624 | tf_op jit(solution)/shard_map/all_gather | solution.py:95
  204.8 10.9 %multiply_convert_fusion.1 = (bf16[512,4096]{1,0:T(8,128)(2,1)}, f32[512,4096]{1,0:T(8,128)}) fusion(f32[4096]{0:T(1024)S(1)} %bitcast.241, bf16[1024,4096]{1,0:T(8,128)(2,1)} %all-gather.9.cloned.1.call-done, f32[512,1024]{1,0:T(8,128)S(1)} %get-tuple-element.69, f32[1024]{0:T(1024)S(1)} %get-tuple-element.57, f32[1024]{0:T(1024)S(1)} %get-tuple-element.58, ...), kind=kOutput, calls=%fused_computation.16 | convolution fusion | flops 4310171648 | bytes 23097344 | tf_op jit(solution)/shard_map/dot_general | solution.py:15
  215.8 45.2 %all-gather.11.cloned.1.call-done = bf16[4096,1024]{1,0:T(8,128)(2,1)} async-done(((bf16[512,1024]{1,0:T(8,128)(2,1)}), bf16[4096,1024]{1,0:T(8,128)(2,1)}) %all-gather.11.cloned.1.call-update) | async-done | bytes 8388624 | tf_op jit(solution)/shard_map/all_gather | solution.py:95
  261.0 8.5 %fusion.103 = (f32[512]{0:T(512)S(1)}, f32[512,1024]{1,0:T(8,128)S(1)}) fusion(f32[1024]{0:T(1024)S(1)} %get-tuple-element.56, bf16[512,4096]{1,0:T(8,128)(2,1)} %get-tuple-element.70, bf16[4096,1024]{1,0:T(8,128)(2,1)} %all-gather.11.cloned.1.call-done, f32[1024]{0:T(1024)S(1)} %get-tuple-element.57, f32[1024]{0:T(1024)S(1)} %get-tuple-element.58, ...), kind=kOutput, calls=%fused_computation.175 | convolution fusion | flops 4298636800 | bytes 16795648 | tf_op jit(solution)/shard_map/dot_general | solution.py:15
  270.7 2.2 fusion.95
  273.0 11.9 %convert_reduce_fusion = (f32[4096]{0:T(1024)S(1)}, bf16[512,4096]{1,0:T(8,128)(2,1)S(1)}) fusion(f32[512,4096]{1,0:T(8,128)} %get-tuple-element.71, f32[4096]{0:T(1024)S(1)} %bitcast.242, bf16[4096,1024]{1,0:T(8,128)(2,1)} %all-gather.11.cloned.1.call-done, f32[512,1024]{1,0:T(8,128)S(1)} %get-tuple-element.30), kind=kOutput, calls=%fused_computation.12 | convolution fusion | flops 4322750464 | bytes 23101440 | tf_op jit(solution)/shard_map/dot_general | solution.py:23
  285.0 5.2 multiply_reduce_fusion.2
  290.9 1.3 copy-done.3
  292.3 2.3 convolution_convert_fusion.6
  294.5 2.4 copy.77
  296.9 2.1 reshape.336
  299.0 5.8 fusion.55
  304.8 13.5 %fusion.44 = bf16[2,256,16,64]{1,3,2,0:T(8,128)(2,1)} fusion(f32[2,16,256,256]{2,3,1,0:T(8,128)} %fusion.55, bf16[2,256,16,64]{1,0,3,2:T(2,128)(2,1)} %reshape.331, f32[2,16,256,256]{2,3,1,0:T(8,128)} %copy-done.41, f32[2,16,256]{2,1,0:T(8,128)S(1)} %get-tuple-element.66), kind=kOutput, calls=%fused_computation.72 | convolution fusion | flops 283648256 | bytes 18907136 | tf_op jit(solution)/shard_map/bhqk,bhqd->bhkd/dot_general | solution.py:189
  318.3 13.3 %convert_reduce_fusion.2 = (f32[16,64]{1,0:T(8,128)S(1)}, bf16[2,256,16,64]{1,3,2,0:T(8,128)(2,1)}) fusion(f32[2,16,256,256]{2,3,1,0:T(8,128)} %fusion.55, f32[2,16,256,256]{2,3,1,0:T(8,128)} %copy-done.41, f32[2,16,256]{2,1,0:T(8,128)S(1)} %get-tuple-element.66, bf16[2,256,16,64]{1,0,3,2:T(2,128)(2,1)S(1)} %copy-done.11), kind=kOutput, calls=%fused_computation.33 | convolution fusion | flops 284695808 | bytes 18911232 | tf_op jit(solution)/shard_map/bhqk,bhkd->bhqd/dot_general | solution.py:186
  331.6 5.2 convert_reduce_fusion.1
  342.4 1.3 convolution_convert_fusion.3
  343.7 1.3 convolution_convert_fusion.4
  345.1 1.3 convolution_convert_fusion.5
  346.4 3.7 pad_maximum_fusion
  350.1 9.8 %convolution_convert_fusion.1 = bf16[1024,4096]{1,0:T(8,128)(2,1)} fusion(bf16[512,4096]{1,0:T(8,128)(2,1)} %copy-done.42, f32[512,1024]{1,0:T(8,128)S(1)} %get-tuple-element.69, f32[1024]{0:T(1024)S(1)} %get-tuple-element.57, f32[1024]{0:T(1024)S(1)} %get-tuple-element.58, f32[512]{0:T(512)S(1)} %add_rsqrt_fusion.1, f32[512]{0:T(512)S(1)} %broadcast_multiply_fusion.4), kind=kOutput, calls=%fused_computation.21 | convolution fusion | flops 4301783040 | bytes 14692352 | tf_op jit(solution)/shard_map/dot_general | solution.py:19
  360.0 2.0 copy-done.17
  362.0 9.9 %convolution_convert_fusion = bf16[4096,1024]{1,0:T(8,128)(2,1)} fusion(bf16[512,4096]{1,0:T(8,128)(2,1)} %get-tuple-element.70, f32[512,1024]{1,0:T(8,128)S(1)} %copy-done.17), kind=kOutput, calls=%fused_computation.20 | convolution fusion | flops 4299685888 | bytes 14680064 | tf_op jit(solution)/shard_map/dot_general | solution.py:19
  377.3 44.2 %reduce-scatter.4.cloned.1.call-done = bf16[512,1024]{1,0:T(8,128)(2,1)} async-done(((bf16[4096,1024]{1,0:T(8,128)(2,1)}), bf16[512,1024]{1,0:T(8,128)(2,1)}) %reduce-scatter.4.cloned.1.call-update) | async-done | bytes 1048592 | tf_op jit(solution)/shard_map/reduce_scatter | solution.py:165
  421.6 75.0 %reduce-scatter.6.cloned.1.call-done = bf16[128,4096]{1,0:T(8,128)(2,1)} async-done(((bf16[1024,4096]{1,0:T(8,128)(2,1)}), bf16[128,4096]{1,0:T(8,128)(2,1)}) %reduce-scatter.6.cloned.1.call-update) | async-done | bytes 1048592 | tf_op jit(solution)/shard_map/reduce_scatter | solution.py:165
  496.6 74.7 %reduce-scatter.8.cloned.1.call-done = bf16[512,1024]{1,0:T(8,128)(2,1)} async-done(((bf16[4096,1024]{1,0:T(8,128)(2,1)}), bf16[512,1024]{1,0:T(8,128)(2,1)}) %reduce-scatter.8.cloned.1.call-update) | async-done | bytes 1048592 | tf_op jit(solution)/shard_map/reduce_scatter | solution.py:165
  571.4 43.1 %psum.29 = f32[8,1536]{1,0:T(8,128)S(1)} all-reduce(f32[8,1536]{1,0:T(8,128)S(1)} %constant_dynamic-update-slice_fusion), channel_id=1, replica_groups=mesh['shard'=8,'rep'=4] {'shard','rep'}, use_global_device_ids=true, to_apply=%region_23.25 | all-reduce | flops 12288 | bytes 98304 | tf_op jit(solution)/shard_map/psum | solution.py:227
  615.9 2.7 fusion.107
  620.9 2.3 add_convert_fusion
  623.2 31.6 %all-gather.13.cloned.1.call-done = bf16[8,256,1024]{2,1,0:T(8,128)(2,1)} async-done(((bf16[2,256,1024]{2,1,0:T(8,128)(2,1)}), bf16[8,256,1024]{2,1,0:T(8,128)(2,1)}) %all-gather.13.cloned.1.call-update) | async-done | bytes 4194320 | tf_op jit(solution)/shard_map/all_gather | solution.py:156
  657.2 120.7 %all-reduce.3.cloned.1.call-done = (bf16[512,1024]{1,0:T(8,128)(2,1)}, bf16[128,4096]{1,0:T(8,128)(2,1)}, bf16[512,1024]{1,0:T(8,128)(2,1)}) async-done(((bf16[512,1024]{1,0:T(8,128)(2,1)}, bf16[128,4096]{1,0:T(8,128)(2,1)}, bf16[512,1024]{1,0:T(8,128)(2,1)}), (bf16[512,1024]{1,0:T(8,128)(2,1)}, bf16[128,4096]{1,0:T(8,128)(2,1)}, bf16[512,1024]{1,0:T(8,128)(2,1)})) %all-reduce.3.cloned.1.call-update) | async-done | bytes 3145744 | tf_op jit(solution)/shard_map/psum | solution.py:168
  777.8 2.7 fusion.98
  780.5 1.5 convert_element_type.284
  782.0 1.6 convert_element_type.286
  (175 shorter events, 27.3 us)
Async XLA Ops:
  7.2 21.6 %copy-start = (s32[64]{0:T(128)S(1)}, s32[64]{0:T(128)}, u32[]{:S(2)}) copy-start(s32[64]{0:T(128)} %param.22) | copy-start | bytes 772
  7.2 86.0 %all-gather.15.cloned.1.call-start = ((), (), s32[]{:S(2)}) async-start(), calls=%async_computation.7 | async-start | bytes 5242880 | tf_op jit(solution)/shard_map/all_gather | solution.py:123
  7.9 140.6 %all-gather.7.cloned.1.call-start = ((), (), s32[]{:S(2)}) async-start(), calls=%async_computation.3 | async-start | bytes 9437184 | tf_op jit(solution)/shard_map/all_gather | solution.py:95
  10.2 6.1 copy-start.33
  10.2 6.4 copy-start.34
  10.2 6.6 copy-start.35
  10.2 6.8 copy-start.36
  10.2 7.0 copy-start.37
  10.3 7.2 copy-start.38
  10.3 7.4 copy-start.39
  10.3 7.6 copy-start.40
  10.3 7.8 copy-start.32
  10.3 194.5 %all-gather.9.cloned.1.call-start = ((), (), s32[]{:S(2)}) async-start(), calls=%async_computation.4 | async-start | bytes 9437184 | tf_op jit(solution)/shard_map/all_gather | solution.py:95
  11.1 249.9 %all-gather.11.cloned.1.call-start = ((), (), s32[]{:S(2)}) async-start(), calls=%async_computation.5 | async-start | bytes 9437184 | tf_op jit(solution)/shard_map/all_gather | solution.py:95
  11.6 409.9 %reduce-scatter.4.cloned.1.call-start = ((), (), s32[]{:S(2)}) async-start(), calls=%async_computation.8 | async-start | bytes 9437184 | tf_op jit(solution)/shard_map/reduce_scatter | solution.py:165
  148.5 7.3 copy-start.27
  157.4 18.8 %copy-start.12 = (bf16[2,256,16,64]{1,0,3,2:T(2,128)(2,1)}, bf16[2,256,16,64]{1,0,3,2:T(2,128)(2,1)S(1)}, u32[]{:S(2)}) copy-start(bf16[2,256,16,64]{1,0,3,2:T(2,128)(2,1)S(1)} %reshape.333) | copy-start | bytes 3145732
  163.5 6.7 copy-start.10
  176.1 4.2 copy-start.41
  180.3 1.6 copy-start.8
  180.3 1.9 copy-start.28
  181.6 1.9 copy-start.14
  270.7 14.2 %slice-start = ((s8[8388608]{0:T(1024)(128)(4,1)}), s8[4194304]{0:T(1024)(128)(4,1)S(1)}, s32[]{:S(2)}) async-start(s8[8388608]{0:T(1024)(128)(4,1)} %bitcast.245), calls=%async_computation.12 | async-start | bytes 8388608
  273.0 12.0 %copy-start.16 = (f32[512,1024]{1,0:T(8,128)}, f32[512,1024]{1,0:T(8,128)S(1)}, u32[]{:S(2)}) copy-start(f32[512,1024]{1,0:T(8,128)S(1)} %get-tuple-element.30) | copy-start | bytes 6291460
  273.0 12.0 %slice-start.1 = ((s8[8388608]{0:T(1024)(128)(4,1)}), s8[4194304]{0:T(1024)(128)(4,1)S(1)}, s32[]{:S(2)}) async-start(s8[8388608]{0:T(1024)(128)(4,1)} %bitcast.245), calls=%async_computation.13 | async-start | bytes 8388608
  284.9 5.3 copy-start.42
  290.2 2.1 copy-start.9
  294.5 4.5 copy-start.13
  304.8 13.5 %copy-start.11 = (bf16[2,256,16,64]{1,0,3,2:T(2,128)(2,1)S(1)}, bf16[2,256,16,64]{1,0,3,2:T(2,128)(2,1)}, u32[]{:S(2)}) copy-start(bf16[2,256,16,64]{1,0,3,2:T(2,128)(2,1)} %copy-done.10) | copy-start | bytes 3145732
  331.5 5.3 copy-start.4
  331.6 5.3 copy-start.15
  339.4 4.3 copy-start.22
  340.8 4.2 copy-start.23
  340.8 1.6 copy-start.29
  350.1 146.5 %reduce-scatter.6.cloned.1.call-start = ((), (), s32[]{:S(2)}) async-start(), calls=%async_computation.9 | async-start | bytes 9437184 | tf_op jit(solution)/shard_map/reduce_scatter | solution.py:165
  359.9 2.0 copy-start.17
  360.0 211.4 %reduce-scatter.8.cloned.1.call-start = ((), (), s32[]{:S(2)}) async-start(), calls=%async_computation.10 | async-start | bytes 9437184 | tf_op jit(solution)/shard_map/reduce_scatter | solution.py:165
  371.9 282.9 %all-gather.13.cloned.1.call-start = ((), (), s32[]{:S(2)}) async-start(), calls=%async_computation.6 | async-start | bytes 5242880 | tf_op jit(solution)/shard_map/all_gather | solution.py:156
  371.9 199.5 %copy-start.30 = (f32[1024]{0:T(1024)S(1)}, f32[1024]{0:T(1024)}, u32[]{:S(2)}) copy-start(f32[1024]{0:T(1024)} %get-tuple-element.24) | copy-start | bytes 12292
  371.9 243.9 %copy-start.19 = (bf16[8,1,128,1024]{3,2,1,0:T(8,128)(2,1)S(1)}, bf16[8,1,128,1024]{3,2,1,0:T(8,128)(2,1)}, u32[]{:S(2)}) copy-start(bf16[8,1,128,1024]{3,2,1,0:T(8,128)(2,1)} %get-tuple-element.35) | copy-start | bytes 6291460
  372.6 405.2 %all-reduce.3.cloned.1.call-start = ((), (), s32[]{:S(2)}) async-start(), calls=%async_computation.11 | async-start | bytes 6291456 | tf_op jit(solution)/shard_map/psum | solution.py:168
  615.9 2.7 copy-start.18
  615.9 2.7 copy-start.24
  618.6 1.6 copy-start.5
  618.6 2.2 copy-start.7
  777.8 2.7 copy-start.21
  780.5 1.5 copy-start.20
  780.5 3.1 copy-start.1
  (6 other events, 7.7 us)
Sparse Core Ops, SparseCore 0:
  9.6 83.5 all-gather.14
  95.6 52.8 all-gather.6
  150.4 54.3 all-gather.8
  206.6 54.3 all-gather.10
  350.2 71.2 reduce-scatter.3
  425.3 71.2 reduce-scatter.5
  500.0 71.2 reduce-scatter.7
  573.0 81.7 all-gather.12
  657.6 120.2 all-reduce.2
where the time goes:
time: 794 us; the launch traced here: 790 us
  waiting for transfers between devices  530 us (67%)
  matrix products  123 us (15%)
  blocking collectives  53.8 us (7%)
  local copies, waits for them, and re-layouts  40.2 us (5%)
  between operations  22.6 us (3%)
  other arithmetic  20 us (3%)
    reduce_scatter x3, waiting for transfers between devices, reduced(): return lax.psum_scatter(part, 'shard', scatter_dimension=0, tiled=True)  194 us
    psum x1, waiting for transfers between devices, over_rep(): return lax.psum(part, 'rep').astype(F32)  121 us
    all_gather x3, waiting for transfers between devices, gather(): return lax.all_gather(block, 'shard', axis=0, tiled=True)  119 us
    all_gather x1, waiting for transfers between devices, local(): cot = pick(lax.all_gather(cotangent, 'rep', axis=0, tiled=True), wanted)  62.3 us
    psum x1, blocking collectives, local(): g_vec = lax.psum(g_vec, ('shard', 'rep'))  43.1 us
    all_gather x1, waiting for transfers between devices, local(): layer_out = pick(lax.all_gather(out, 'rep', axis=0, tiled=True), sources)  31.6 us
    dot_general x6, matrix products, matmul(): return jnp.dot(left, right, preferred_element_type=F32)  31.3 us
    dot_general x6, matrix products, right_trans(): lax.dot_general(left, right, (((1,), (1,)), ((), ())), preferred_element_...  25.8 us
  transfers between devices with their start and end apart: 9, of which 9 were waited for; matrix products, arithmetic and copies ran while one was open for 10% of the time, Pallas kernels for 0%

commit v1 on v0

--- a/solution.py
+++ b/solution.py
@@ -92,7 +92,9 @@
     )
 
     def gather(block):
-        return lax.all_gather(block, "shard", axis=0, tiled=True)
+        return jnp.concatenate(
+            lax.all_to_all(jnp.stack([block] * lax.axis_size("shard")), "shard", 0, 0), axis=0
+        )
 
     block = w_query.shape[0]
     wide = w_up.shape[1]

time: 794 us -> 799 us (level)
  waiting for transfers between devices: 530 us -> 337 us
  blocking collectives: 53.8 us -> 231 us
  starting transfers between devices: 0.36 us -> 10.7 us
    all_gather x3 -> x0, waiting for transfers between devices: 119 us -> none  [gather(): return lax.all_gather(block, 'shard', axis=0, tiled=True)]
    all_to_all x0 -> x1, blocking collectives: none -> 99.2 us  [gather(): lax.all_to_all(jnp.stack([block] * lax.axis_size('shard')), 'shard', 0, 0)]
    all_gather x1, blocking collectives: 10.6 us -> 89.2 us  [local(): lax.all_gather(vec, 'shard', axis=0, tiled=True).reshape(shards, -1)]
    all_gather x1, waiting for transfers between devices: 62.3 us -> 0.02 us  [local(): cot = pick(lax.all_gather(cotangent, 'rep', axis=0, tiled=True), wanted)]
    reduce_scatter x3, waiting for transfers between devices: 194 us -> 134 us  [reduced(): return lax.psum_scatter(part, 'shard', scatter_dimension=0, tiled=True)]
    all_to_all x0 -> x2, waiting for transfers between devices: none -> 49.6 us  [gather(): lax.all_to_all(jnp.stack([block] * lax.axis_size('shard')), 'shard', 0, 0)]
    all_to_all x0 -> x2, starting transfers between devices: none -> 10 us  [gather(): lax.all_to_all(jnp.stack([block] * lax.axis_size('shard')), 'shard', 0, 0)]
    another operation x0 -> x3, local copies, waits for them, and re-layouts: none -> 9.64 us  [gather(): jnp.stack([block] * lax.axis_size('shard'))]
  transfers between devices with their start and end apart: 9 -> 8, of which waited for: 9 -> 5; matrix products, arithmetic and copies ran while one was open for 10% -> 17% of each run, Pallas kernels for 0% -> 0%
where the time goes in v1:
time: 799 us; the launch traced here: 793 us
  waiting for transfers between devices  337 us (42%)
  blocking collectives  231 us (29%)
  matrix products  124 us (16%)
  local copies, waits for them, and re-layouts  47.8 us (6%)
  between operations  23.2 us (3%)
  other arithmetic  19 us (2%)
  starting transfers between devices  10.7 us (1%)
    reduce_scatter x3, waiting for transfers between devices, reduced(): return lax.psum_scatter(part, 'shard', scatter_dimension=0, tiled=True)  134 us
    psum x1, waiting for transfers between devices, over_rep(): return lax.psum(part, 'rep').astype(F32)  121 us
    all_to_all x1, blocking collectives, gather(): lax.all_to_all(jnp.stack([block] * lax.axis_size('shard')), 'shard', 0, 0)  99.2 us
    all_gather x1, blocking collectives, local(): lax.all_gather(vec, 'shard', axis=0, tiled=True).reshape(shards, -1)  89.2 us
    all_to_all x2, waiting for transfers between devices, gather(): lax.all_to_all(jnp.stack([block] * lax.axis_size('shard')), 'shard', 0, 0)  49.6 us
    psum x1, blocking collectives, local(): g_vec = lax.psum(g_vec, ('shard', 'rep'))  43 us
    all_gather x1, waiting for transfers between devices, local(): layer_out = pick(lax.all_gather(out, 'rep', axis=0, tiled=True), sources)  31.6 us
    dot_general x6, matrix products, matmul(): return jnp.dot(left, right, preferred_element_type=F32)  29.9 us
  transfers between devices with their start and end apart: 8, of which 5 were waited for; matrix products, arithmetic and copies ran while one was open for 17% of the time, Pallas kernels for 0%

profile of v1, /device:TPU:0, one launch (start us, length us, event | category | flops | bytes accessed | tf_op | source)
XLA Modules:
  0.0 793.4 jit_solution(17717771658266713669)
XLA Ops:
  9.6 99.2 %all_to_all.15 = bf16[8,512,1024]{2,1,0:T(8,128)(2,1)} all-to-all(bf16[8,512,1024]{2,1,0:T(8,128)(2,1)S(1)} %stack.10), channel_id=1, replica_groups=mesh['shard'=8,'rep'=4] {'shard'}, dimensions={0} | all-to-all | bytes 16777216 | tf_op jit(solution)/shard_map/all_to_all | solution.py:96
  108.8 4.3 stack.11
  113.1 5.1 all-to-all-start.1
  126.2 89.2 %all-gather = bf16[8,1,1536]{2,1,0:T(2,128)(2,1)S(1)} all-gather(bf16[1,1,1536]{2,1,0:T(2,128)(2,1)S(1)} %reshape.393), channel_id=1, replica_groups=mesh['shard'=8,'rep'=4] {'shard'}, dimensions={0}, use_global_device_ids=true | all-gather | bytes 27648 | tf_op jit(solution)/shard_map/all_gather | solution.py:104
  216.8 1.3 constant_dynamic-slice_fusion.2
  218.1 4.3 stack.12
  222.4 5.0 all-to-all-start.2
  228.7 5.8 fusion.97
  234.5 1.3 copy-done.5
  235.8 1.3 fusion.54
  237.4 3.5 fusion.53
  242.0 4.1 fusion.43
  246.2 1.3 reshape.340
  247.5 2.9 fusion.59
  250.4 3.5 fusion.101
  254.8 2.4 copy-done.39
  259.0 1.4 fusion.102
  260.8 11.0 %multiply_convert_fusion.1 = (bf16[512,4096]{1,0:T(8,128)(2,1)}, f32[512,4096]{1,0:T(8,128)}) fusion(f32[4096]{0:T(1024)S(1)} %bitcast.243, bf16[1024,4096]{1,0:T(8,128)(2,1)} %bitcast.18, f32[512,1024]{1,0:T(8,128)S(1)} %get-tuple-element.69, f32[1024]{0:T(1024)S(1)} %get-tuple-element.57, f32[1024]{0:T(1024)S(1)} %get-tuple-element.58, ...), kind=kOutput, calls=%fused_computation.16 | convolution fusion | flops 4310171648 | bytes 23097344 | tf_op jit(solution)/shard_map/dot_general | solution.py:15
  271.8 49.6 %all-to-all-done.2 = bf16[8,512,1024]{2,1,0:T(8,128)(2,1)} async-done(((bf16[8,512,1024]{2,1,0:T(8,128)(2,1)}), bf16[8,512,1024]{2,1,0:T(8,128)(2,1)}, u32[]{:S(2)}, u32[]{:S(2)}) %all-to-all-start.2) | async-done | bytes 8388640 | tf_op jit(solution)/shard_map/all_to_all | solution.py:96
  321.4 8.5 %fusion.103 = (f32[512]{0:T(512)S(1)}, f32[512,1024]{1,0:T(8,128)S(1)}) fusion(f32[1024]{0:T(1024)S(1)} %get-tuple-element.56, bf16[512,4096]{1,0:T(8,128)(2,1)} %get-tuple-element.70, bf16[4096,1024]{1,0:T(8,128)(2,1)} %bitcast.19, f32[1024]{0:T(1024)S(1)} %get-tuple-element.57, f32[1024]{0:T(1024)S(1)} %get-tuple-element.58, ...), kind=kOutput, calls=%fused_computation.175 | convolution fusion | flops 4298636800 | bytes 16795648 | tf_op jit(solution)/shard_map/dot_general | solution.py:15
  331.1 2.2 fusion.95
  334.0 10.0 %convert_reduce_fusion = (f32[4096]{0:T(1024)S(1)}, bf16[512,4096]{1,0:T(8,128)(2,1)S(1)}) fusion(f32[512,4096]{1,0:T(8,128)S(1)} %copy-done.40, f32[4096]{0:T(1024)S(1)} %bitcast.244, bf16[4096,1024]{1,0:T(8,128)(2,1)} %bitcast.19, f32[512,1024]{1,0:T(8,128)S(1)} %get-tuple-element.30), kind=kOutput, calls=%fused_computation.12 | convolution fusion | flops 4322750464 | bytes 23101440 | tf_op jit(solution)/shard_map/dot_general | solution.py:23
  344.0 2.0 copy-done.41
  346.1 7.4 convolution_convert_fusion.1
  353.8 12.0 %convolution_convert_fusion = bf16[4096,1024]{1,0:T(8,128)(2,1)} fusion(bf16[512,4096]{1,0:T(8,128)(2,1)} %get-tuple-element.70, f32[512,1024]{1,0:T(8,128)} %copy-done.16), kind=kOutput, calls=%fused_computation.20 | convolution fusion | flops 4299685888 | bytes 14680064 | tf_op jit(solution)/shard_map/dot_general | solution.py:19
  365.9 11.5 %multiply_reduce_fusion.2 = (f32[1024]{0:T(1024)S(1)}, f32[512]{0:T(512)S(1)}, f32[512]{0:T(512)S(1)}, f32[1024]{0:T(1024)S(1)}, f32[512,1024]{1,0:T(8,128)S(1)}) fusion(f32[512,1024]{1,0:T(8,128)S(1)} %get-tuple-element.69, f32[512]{0:T(512)S(1)} %add_rsqrt_fusion.1, f32[512]{0:T(512)S(1)} %broadcast_multiply_fusion.4, f32[1024]{0:T(1024)S(1)} %get-tuple-element.58, ...), kind=kOutput, calls=%fused_computation.31 | convolution fusion | flops 4300207104 | bytes 18894848 | tf_op jit(solution)/shard_map/dot_general | solution.py:23
  378.1 1.3 copy-done.3
  380.1 1.3 convolution_convert_fusion.6
  382.4 5.2 convert_reduce_fusion.1
  389.0 4.5 fusion.55
  393.5 13.5 %fusion.44 = bf16[2,256,16,64]{1,3,2,0:T(8,128)(2,1)} fusion(f32[2,16,256,256]{2,3,1,0:T(8,128)} %fusion.55, bf16[2,256,16,64]{1,0,3,2:T(2,128)(2,1)S(1)} %copy-done.13, f32[2,16,256,256]{2,3,1,0:T(8,128)} %copy-done.39, f32[2,16,256]{2,1,0:T(8,128)S(1)} %get-tuple-element.66), kind=kOutput, calls=%fused_computation.72 | convolution fusion | flops 283648256 | bytes 18907136 | tf_op jit(solution)/shard_map/bhqk,bhqd->bhkd/dot_general | solution.py:191
  407.0 2.4 copy.82
  410.6 12.6 %convert_reduce_fusion.2 = (f32[16,64]{1,0:T(8,128)S(1)}, bf16[2,256,16,64]{1,3,2,0:T(8,128)(2,1)S(1)}) fusion(f32[2,16,256,256]{2,3,1,0:T(8,128)} %fusion.55, f32[2,16,256,256]{2,3,1,0:T(8,128)} %copy-done.39, f32[2,16,256]{2,1,0:T(8,128)S(1)} %get-tuple-element.66, bf16[2,256,16,64]{1,0,3,2:T(2,128)(2,1)S(1)} %copy-done.10), kind=kOutput, calls=%fused_computation.33 | convolution fusion | flops 284695808 | bytes 18911232 | tf_op jit(solution)/shard_map/bhqk,bhkd->bhqd/dot_general | solution.py:188
  424.6 1.3 convolution_convert_fusion.3
  426.2 1.3 convolution_convert_fusion.4
  427.5 1.3 convolution_convert_fusion.5
  430.6 3.7 pad_maximum_fusion
  439.7 59.8 %reduce-scatter.8.cloned.1.call-done = bf16[512,1024]{1,0:T(8,128)(2,1)} async-done(((bf16[4096,1024]{1,0:T(8,128)(2,1)}), bf16[512,1024]{1,0:T(8,128)(2,1)}) %reduce-scatter.8.cloned.1.call-update) | async-done | bytes 1048592 | tf_op jit(solution)/shard_map/reduce_scatter | solution.py:167
  499.5 74.6 %reduce-scatter.4.cloned.1.call-done = bf16[512,1024]{1,0:T(8,128)(2,1)} async-done(((bf16[4096,1024]{1,0:T(8,128)(2,1)}), bf16[512,1024]{1,0:T(8,128)(2,1)}) %reduce-scatter.4.cloned.1.call-update) | async-done | bytes 1048592 | tf_op jit(solution)/shard_map/reduce_scatter | solution.py:167
  574.2 43.0 %psum.29 = f32[8,1536]{1,0:T(8,128)S(1)} all-reduce(f32[8,1536]{1,0:T(8,128)S(1)} %constant_dynamic-update-slice_fusion), channel_id=1, replica_groups=mesh['shard'=8,'rep'=4] {'shard','rep'}, use_global_device_ids=true, to_apply=%region_23.25 | all-reduce | flops 12288 | bytes 98304 | tf_op jit(solution)/shard_map/psum | solution.py:229
  618.5 3.4 fusion.107
  622.0 1.3 fusion.106
  623.6 2.3 add_convert_fusion
  625.9 31.6 %all-gather.4.cloned.1.call-done = bf16[8,256,1024]{2,1,0:T(8,128)(2,1)} async-done(((bf16[2,256,1024]{2,1,0:T(8,128)(2,1)}), bf16[8,256,1024]{2,1,0:T(8,128)(2,1)}) %all-gather.4.cloned.1.call-update) | async-done | bytes 4194320 | tf_op jit(solution)/shard_map/all_gather | solution.py:158
  659.8 120.5 %all-reduce.3.cloned.1.call-done = (bf16[512,1024]{1,0:T(8,128)(2,1)}, bf16[128,4096]{1,0:T(8,128)(2,1)}, bf16[512,1024]{1,0:T(8,128)(2,1)}) async-done(((bf16[512,1024]{1,0:T(8,128)(2,1)}, bf16[128,4096]{1,0:T(8,128)(2,1)}, bf16[512,1024]{1,0:T(8,128)(2,1)}), (bf16[512,1024]{1,0:T(8,128)(2,1)}, bf16[128,4096]{1,0:T(8,128)(2,1)}, bf16[512,1024]{1,0:T(8,128)(2,1)})) %all-reduce.3.cloned.1.call-update) | async-done | bytes 3145744 | tf_op jit(solution)/shard_map/psum | solution.py:170
  780.3 2.7 fusion.98
  783.0 1.5 convert_element_type.284
  784.5 1.6 convert_element_type.286
  (167 shorter events, 29.2 us)
Async XLA Ops:
  7.2 116.5 %copy-start = (s32[64]{0:T(128)S(1)}, s32[64]{0:T(128)}, u32[]{:S(2)}) copy-start(s32[64]{0:T(128)} %param.22) | copy-start | bytes 772
  9.6 99.2 %copy-start.18 = (bf16[128,4096]{1,0:T(8,128)(2,1)S(1)}, bf16[128,4096]{1,0:T(8,128)(2,1)}, u32[]{:S(2)}) copy-start(bf16[128,4096]{1,0:T(8,128)(2,1)} %param.33) | copy-start | bytes 3145732
  113.1 6.0 copy-start.2
  113.1 105.0 %all-to-all-start.1 = ((bf16[8,128,4096]{2,1,0:T(8,128)(2,1)}), bf16[8,128,4096]{2,1,0:T(8,128)(2,1)}, u32[]{:S(2)}, u32[]{:S(2)}) async-start(bf16[8,128,4096]{2,1,0:T(8,128)(2,1)} %stack.11), calls=%async_computation.1 | async-start | bytes 16777216 | tf_op jit(solution)/shard_map/all_to_all | solution.py:96
  118.1 6.3 copy-start.31
  118.1 6.5 copy-start.32
  118.2 6.7 copy-start.33
  118.2 6.9 copy-start.34
  118.2 7.1 copy-start.35
  118.2 7.3 copy-start.36
  118.2 7.5 copy-start.37
  118.2 7.7 copy-start.38
  118.2 7.9 %copy-start.30 = (bf16[512]{0:T(512)(128)(2,1)S(1)}, bf16[512]{0:T(512)(128)(2,1)}, u32[]{:S(2)}) copy-start(bf16[512]{0:T(512)(128)(2,1)} %param.34) | copy-start | bytes 3076
  118.2 99.8 %copy-start.19 = (bf16[512,1024]{1,0:T(8,128)(2,1)S(1)}, bf16[512,1024]{1,0:T(8,128)(2,1)}, u32[]{:S(2)}) copy-start(bf16[512,1024]{1,0:T(8,128)(2,1)} %param.35) | copy-start | bytes 3145732
  118.3 98.5 %all-gather.6.cloned.1.call-start = ((), (), s32[]{:S(2)}) async-start(), calls=%async_computation.7 | async-start | bytes 5242880 | tf_op jit(solution)/shard_map/all_gather | solution.py:125
  222.4 99.0 %all-to-all-start.2 = ((bf16[8,512,1024]{2,1,0:T(8,128)(2,1)}), bf16[8,512,1024]{2,1,0:T(8,128)(2,1)}, u32[]{:S(2)}, u32[]{:S(2)}) async-start(bf16[8,512,1024]{2,1,0:T(8,128)(2,1)} %stack.12), calls=%async_computation.2 | async-start | bytes 16777216 | tf_op jit(solution)/shard_map/all_to_all | solution.py:96
  227.4 212.3 %reduce-scatter.6.cloned.1.call-start = ((), (), s32[]{:S(2)}) async-start(), calls=%async_computation.9 | async-start | bytes 9437184 | tf_op jit(solution)/shard_map/reduce_scatter | solution.py:167
  228.7 7.1 copy-start.25
  237.4 16.6 %copy-start.11 = (bf16[2,256,16,64]{1,0,3,2:T(2,128)(2,1)}, bf16[2,256,16,64]{1,0,3,2:T(2,128)(2,1)S(1)}, u32[]{:S(2)}) copy-start(bf16[2,256,16,64]{1,0,3,2:T(2,128)(2,1)S(1)} %reshape.341) | copy-start | bytes 3145732
  247.5 2.9 copy-start.9
  253.9 3.2 copy-start.39
  257.2 1.6 copy-start.7
  257.2 1.9 copy-start.26
  258.5 1.9 copy-start.14
  330.3 3.8 copy-start.40
  333.4 10.7 %copy-start.16 = (f32[512,1024]{1,0:T(8,128)}, f32[512,1024]{1,0:T(8,128)S(1)}, u32[]{:S(2)}) copy-start(f32[512,1024]{1,0:T(8,128)S(1)} %get-tuple-element.30) | copy-start | bytes 6291460
  344.0 2.0 copy-start.41
  353.5 146.0 %reduce-scatter.8.cloned.1.call-start = ((), (), s32[]{:S(2)}) async-start(), calls=%async_computation.10 | async-start | bytes 9437184 | tf_op jit(solution)/shard_map/reduce_scatter | solution.py:167
  365.8 208.3 %reduce-scatter.4.cloned.1.call-start = ((), (), s32[]{:S(2)}) async-start(), calls=%async_computation.8 | async-start | bytes 9437184 | tf_op jit(solution)/shard_map/reduce_scatter | solution.py:167
  377.4 2.7 copy-start.8
  378.1 1.3 copy-start.3
  387.6 1.3 copy-start.12
  388.9 4.5 copy-start.13
  407.0 3.6 copy-start.10
  423.2 1.4 copy-start.27
  424.6 2.9 copy-start.23
  424.6 1.6 copy-start.22
  427.5 1.6 copy-start.4
  427.5 1.8 copy-start.15
  434.3 223.1 %all-gather.4.cloned.1.call-start = ((), (), s32[]{:S(2)}) async-start(), calls=%async_computation.6 | async-start | bytes 5242880 | tf_op jit(solution)/shard_map/all_gather | solution.py:158
  434.4 139.8 %copy-start.28 = (f32[1024]{0:T(1024)S(1)}, f32[1024]{0:T(1024)}, u32[]{:S(2)}) copy-start(f32[1024]{0:T(1024)} %get-tuple-element.24) | copy-start | bytes 12292
  434.9 345.4 %all-reduce.3.cloned.1.call-start = ((), (), s32[]{:S(2)}) async-start(), calls=%async_computation.11 | async-start | bytes 6291456 | tf_op jit(solution)/shard_map/psum | solution.py:170
  618.5 3.4 copy-start.17
  618.5 3.4 copy-start.24
  622.0 1.6 copy-start.6
  780.3 2.7 copy-start.21
  783.0 1.5 copy-start.20
  783.0 3.1 copy-start.1
  (2 other events, 2.0 us)
Sparse Core Ops, SparseCore 0:
  120.7 82.3 all-gather.5
  353.7 70.6 reduce-scatter.5
  428.2 71.2 reduce-scatter.7
  502.8 71.2 reduce-scatter.3
  575.6 81.7 all-gather.3
  660.1 120.1 all-reduce.2
